TPU v7x, 32 devices: a whole 2x2x4 slice. The times are simulated.
32 devices in a mesh: groups: 2 (over x), win: 16 (over z, y, core).
Axes of the slice: x: 2, y: 2, z: 4, core: 2. Of those that a mesh axis runs over, the one named last changes fastest.
Arguments:
- latents: bfloat16 [6, 8, 256, 1536], P('groups', None, 'win'), parts along dimension 0, may hold values from -60 to 60
- offsets: int32 [6], P('groups'), parts along dimension 0, may hold values from 0 to 8, as said below
- levels: int32 [6], P('groups'), parts along dimension 0, may hold values from 0 to 31
- mod_table: bfloat16 [32, 6, 1536], replicated, may hold values from -3 to 3
- rel_bias: float32 [6, 64, 64], replicated, may hold values from -3 to 403
- w_qkv: bfloat16 [1536, 2304], P('win'), may hold values from -0.15625 to 0.15625
- w_out: bfloat16 [768, 1536], P('win'), may hold values from -0.21875 to 0.21875
- w_up: bfloat16 [1536, 3072], P('win'), may hold values from -0.15625 to 0.15625
- w_down: bfloat16 [3072, 1536], P('win'), may hold values from -0.109375 to 0.109375
Outputs:
- result: bfloat16 [6, 8, 256, 1536], P('groups', None, 'win'), parts along dimension 0
There are 2 independent parts, one for each index of `groups`. A program takes and returns all parts, laid end to end along the dimension named above; an argument that names none is the same for every part. Nothing has to cross between parts.
Inputs may be any that keep to these rules, and one draw needn't show every extreme that they name: `offsets`: some micro-batch has offset 8 in every draw.
All inputs are finite; a program needn't handle non-finite values.
Results may differ from a plain program's by a relative error of at most 0.007.
Values may be sent and summed in bfloat16 or wider, within the bound.
A program may use at most 128 MiB of HBM per device.

v0:
```python
import jax
import jax.numpy as jnp
from jax import lax
from jax.sharding import PartitionSpec as P

HEADS = 6
HEAD_DIM = 128
WIN = 8
LEVELS = 32


def passed_along(shard, axis, by):
    length = lax.axis_size(axis)
    return lax.ppermute(shard, axis, [(i, (i + by) % length) for i in range(length)])


def norm_rows(values_in):
    centre = values_in - jnp.mean(values_in, axis=-1, keepdims=True)
    spread = jnp.mean(centre * centre, axis=-1, keepdims=True)
    return centre * lax.rsqrt(spread + 1e-06)


def restore_grid(region, arrived, offsets, columns):
    widened = jnp.concatenate([region, arrived], axis=2)
    return jax.vmap(lambda plane, shift_by: lax.dynamic_slice_in_dim(plane, shift_by, columns, 1))(
        widened, offsets
    )


def local(latents, offsets, levels, mod_table, rel_bias, w_qkv, w_out, w_up, w_down):
    batches, lat_rows, columns, features = latents.shape
    inner = HEADS * HEAD_DIM
    per_dev = columns // WIN
    selector = (levels[:, None] == jnp.arange(LEVELS, dtype=jnp.int32)[None, :]).astype(
        jnp.bfloat16
    )
    modulation = jnp.dot(
        selector, mod_table.reshape(LEVELS, 6 * features), preferred_element_type=jnp.float32
    )
    modulation = modulation.reshape(batches, 6, 1, 1, features)
    stream = latents.astype(jnp.float32)
    normed = (norm_rows(stream) * (1.0 + modulation[:, 0]) + modulation[:, 1]).astype(jnp.bfloat16)
    arrived = passed_along(normed[:, :, columns - WIN :, :], "win", 1)
    widened = jnp.concatenate([arrived, normed], axis=2)
    rolled = jax.vmap(
        lambda plane, shift_by: lax.dynamic_slice_in_dim(plane, WIN - shift_by, columns, 1)
    )(widened, offsets)
    full_qkv = lax.all_gather(w_qkv, "win", axis=0, tiled=True)
    windows = rolled.reshape(batches, lat_rows, per_dev, WIN, features).transpose(0, 2, 1, 3, 4)
    windows = windows.reshape(-1, lat_rows * WIN, features)
    number = windows.shape[0]
    triple = jnp.dot(windows.reshape(-1, features), full_qkv, preferred_element_type=jnp.float32)
    triple = triple.astype(jnp.bfloat16).reshape(number, lat_rows * WIN, 3, HEADS, HEAD_DIM)
    scores = jnp.einsum(
        "wqhe,wkhe->whqk", triple[:, :, 0], triple[:, :, 1], preferred_element_type=jnp.float32
    )
    scores = scores * (1.0 / HEAD_DIM**0.5) + rel_bias[None]
    probs = jax.nn.softmax(scores, axis=-1).astype(jnp.bfloat16)
    attended = jnp.einsum(
        "whqk,wkhe->wqhe", probs, triple[:, :, 2], preferred_element_type=jnp.float32
    ).astype(jnp.bfloat16)
    attended = attended.reshape(batches, per_dev, lat_rows, WIN, inner).transpose(0, 2, 1, 3, 4)
    attended = attended.reshape(batches, lat_rows, columns, inner)
    full_out = lax.all_gather(w_out, "win", axis=0, tiled=True)
    returned = passed_along(attended[:, :, :WIN, :], "win", -1)
    restored = restore_grid(attended, returned, offsets, columns)
    projected = jnp.dot(restored.reshape(-1, inner), full_out, preferred_element_type=jnp.float32)
    projected = projected.reshape(batches, lat_rows, columns, features)
    middle = (stream + modulation[:, 2] * projected).astype(jnp.bfloat16)
    second = (
        norm_rows(middle.astype(jnp.float32)) * (1.0 + modulation[:, 3]) + modulation[:, 4]
    ).astype(jnp.bfloat16)
    full_up = lax.all_gather(w_up, "win", axis=0, tiled=True)
    hidden = jnp.dot(second.reshape(-1, features), full_up, preferred_element_type=jnp.float32)
    hidden = jax.nn.gelu(hidden, approximate=False).astype(jnp.bfloat16)
    full_down = lax.all_gather(w_down, "win", axis=0, tiled=True)
    lowered = jnp.dot(hidden, full_down, preferred_element_type=jnp.float32).reshape(
        batches, lat_rows, columns, features
    )
    return (middle.astype(jnp.float32) + modulation[:, 5] * lowered).astype(jnp.bfloat16)


def solution(mesh):
    in_specs = (
        P("groups", None, "win", None),
        P("groups"),
        P("groups"),
        P(),
        P(),
        P("win", None),
        P("win", None),
        P("win", None),
        P("win", None),
    )
    out_specs = P("groups", None, "win", None)
    return jax.shard_map(local, mesh=mesh, in_specs=in_specs, out_specs=out_specs, check_vma=False)
```

profile of v0, /device:TPU:5, one launch (start us, length us, event | category | flops | bytes accessed | tf_op | source)
XLA Modules:
  0.0 317.7 jit_solution(2629307609174419920)
XLA Ops:
  6.5 0.7 all-gather.5.cloned.1.call-update
  7.3 0.7 all-gather.7.cloned.1.call-update
  8.1 0.7 all-gather.11.cloned.1.call-update
  8.8 0.5 all-gather.9.cloned.1.call-update
  9.3 0.9 convolution_bitcast_fusion
  10.5 0.4 fusion.22
  11.0 0.7 slice_bitcast_fusion.1
  11.6 0.7 fusion.25
  12.3 0.9 slice.55
  13.2 1.8 collective-permute-start
  15.0 1.7 copy.24
  16.7 9.0 %collective-permute-done = bf16[3,8,8,1536]{3,2,1,0:T(8,128)(2,1)S(1)} collective-permute-done((bf16[3,8,8,1536]{3,2,1,0:T(8,128)(2,1)}, bf16[3,8,8,1536]{3,2,1,0:T(8,128)(2,1)S(1)}, u32[]{:S(2)}, u32[]{:S(2)}) %collective-permute-start) | collective-permute-done | bytes 589856 | tf_op jit(solution)/shard_map/ppermute | solution.py:14
  25.8 0.5 copy.19
  26.3 1.7 gather_fusion
  28.0 2.7 copy.20
  30.7 47.8 %all-gather.5.cloned.1.call-done = bf16[1536,2304]{1,0:T(8,128)(2,1)} async-done(((bf16[96,2304]{1,0:T(8,128)(2,1)}), bf16[1536,2304]{1,0:T(8,128)(2,1)}) %all-gather.5.cloned.1.call-update) | async-done | bytes 7077904 | tf_op jit(solution)/shard_map/all_gather | solution.py:48
  78.4 6.3 %convolution_convert_fusion = bf16[384,2304]{1,0:T(8,128)(2,1)S(1)} fusion(bf16[384,1536]{1,0:T(8,128)(2,1)} %bitcast.93, bf16[1536,2304]{1,0:T(8,128)(2,1)} %all-gather.5.cloned.1.call-done), kind=kOutput, calls=%fused_computation.22 | convolution fusion | flops 2718793728 | bytes 10027008 | tf_op jit(solution)/shard_map/dot_general | solution.py:52
  84.7 3.1 reshape.85
  87.9 3.0 fusion.109
  91.6 2.5 fusion.61
  94.1 1.5 copy.26
  95.5 0.7 reshape.86
  96.4 0.5 collective-permute-start.1
  96.8 6.8 %collective-permute-done.1 = bf16[3,8,8,768]{3,1,0,2:T(8,128)(2,1)S(1)} collective-permute-done((bf16[3,8,8,768]{3,1,0,2:T(8,128)(2,1)S(1)}, bf16[3,8,8,768]{3,1,0,2:T(8,128)(2,1)S(1)}, u32[]{:S(2)}, u32[]{:S(2)}) %collective-permute-start.1) | collective-permute-done | bytes 294944 | tf_op jit(solution)/shard_map/ppermute | solution.py:14
  103.7 0.6 gather_fusion.1
  104.3 17.5 %all-gather.7.cloned.1.call-done = bf16[768,1536]{1,0:T(8,128)(2,1)} async-done(((bf16[48,1536]{1,0:T(8,128)(2,1)}), bf16[768,1536]{1,0:T(8,128)(2,1)}) %all-gather.7.cloned.1.call-update) | async-done | bytes 2359312 | tf_op jit(solution)/shard_map/all_gather | solution.py:64
  121.8 2.9 convert_reduce_fusion
  125.2 0.7 fusion.21
  125.9 77.9 %all-gather.11.cloned.1.call-done = bf16[3072,1536]{1,0:T(8,128)(2,1)} async-done(((bf16[192,1536]{1,0:T(8,128)(2,1)}), bf16[3072,1536]{1,0:T(8,128)(2,1)}) %all-gather.11.cloned.1.call-update) | async-done | bytes 9437200 | tf_op jit(solution)/shard_map/all_gather | solution.py:76
  203.8 81.5 %all-gather.9.cloned.1.call-done = bf16[1536,3072]{1,0:T(8,128)(2,1)} async-done(((bf16[96,3072]{1,0:T(8,128)(2,1)}), bf16[1536,3072]{1,0:T(8,128)(2,1)}) %all-gather.9.cloned.1.call-update) | async-done | bytes 9437200 | tf_op jit(solution)/shard_map/all_gather | solution.py:73
  285.3 22.8 %fusion.16 = f32[384,1536]{1,0:T(8,128)} fusion(bf16[3072,1536]{1,0:T(8,128)(2,1)} %all-gather.11.cloned.1.call-done, bf16[384,1536]{1,0:T(8,128)(2,1)S(1)} %bitcast.92, bf16[1536,3072]{1,0:T(8,128)(2,1)} %all-gather.9.cloned.1.call-done), kind=kOutput, calls=%fused_computation.35 | convolution fusion | flops 7324434432 | bytes 22413312 | tf_op jit(solution)/shard_map/dot_general | solution.py:77
  308.1 3.1 fusion.26
  (31 shorter events, 1.9 us)
Async XLA Ops:
  6.5 2.8 copy-start
  6.5 3.7 %copy-start.1 = (bf16[3,8,16,1536]{3,2,1,0:T(8,128)(2,1)S(1)}, bf16[3,8,16,1536]{3,2,1,0:T(8,128)(2,1)}, u32[]{:S(2)}) copy-start(bf16[3,8,16,1536]{3,2,1,0:T(8,128)(2,1)} %param.9) | copy-start | bytes 3538948
  6.5 71.9 %all-gather.5.cloned.1.call-start = ((), (), s32[]{:S(2)}) async-start(), calls=%async_computation | async-start | bytes 7520256 | tf_op jit(solution)/shard_map/all_gather | solution.py:48
  7.3 114.5 %all-gather.7.cloned.1.call-start = ((), (), s32[]{:S(2)}) async-start(), calls=%async_computation.1 | async-start | bytes 2506752 | tf_op jit(solution)/shard_map/all_gather | solution.py:64
  8.0 195.8 %all-gather.11.cloned.1.call-start = ((), (), s32[]{:S(2)}) async-start(), calls=%async_computation.3 | async-start | bytes 10027008 | tf_op jit(solution)/shard_map/all_gather | solution.py:76
  8.7 276.5 %all-gather.9.cloned.1.call-start = ((), (), s32[]{:S(2)}) async-start(), calls=%async_computation.2 | async-start | bytes 10027008 | tf_op jit(solution)/shard_map/all_gather | solution.py:73
  10.9 5.8 %copy-start.6 = (s32[3]{0:T(128)S(1)}, s32[3]{0:T(128)}, u32[]{:S(2)}) copy-start(s32[3]{0:T(128)} %param.10) | copy-start | bytes 40
  13.2 12.5 %collective-permute-start = (bf16[3,8,8,1536]{3,2,1,0:T(8,128)(2,1)}, bf16[3,8,8,1536]{3,2,1,0:T(8,128)(2,1)S(1)}, u32[]{:S(2)}, u32[]{:S(2)}) collective-permute-start(bf16[3,8,8,1536]{3,2,1,0:T(8,128)(2,1)} %slice.55), channel_id=1, source_target_pairs={{0,1},{1,2},{2,3},{3,4},{4,5},{5,6},{6,7},{7,8},{8,9},{9,10},{10,1... | collective-permute-start | bytes 1769480 | tf_op jit(solution)/shard_map/ppermute | solution.py:14
  87.9 3.0 copy-start.2
  96.4 7.3 %collective-permute-start.1 = (bf16[3,8,8,768]{3,1,0,2:T(8,128)(2,1)S(1)}, bf16[3,8,8,768]{3,1,0,2:T(8,128)(2,1)S(1)}, u32[]{:S(2)}, u32[]{:S(2)}) collective-permute-start(bf16[3,8,8,768]{3,1,0,2:T(8,128)(2,1)S(1)} %slice.59), channel_id=1, source_target_pairs={{0,15},{1,0},{2,1},{3,2},{4,3},{5,4},{6,5},{7,6},{8,7},{9,8},{10,9... | collective-permute-start | bytes 884744 | tf_op jit(solution)/shard_map/ppermute | solution.py:14
  121.8 3.4 %copy-start.4 = (f32[3,1536]{1,0:T(4,128)S(1)}, f32[3,1536]{1,0:T(4,128)}, u32[]{:S(2)}) copy-start(f32[3,1536]{1,0:T(4,128)} %get-tuple-element.9) | copy-start | bytes 55300
  121.8 3.4 %copy-start.5 = (f32[3,1536]{1,0:T(4,128)S(1)}, f32[3,1536]{1,0:T(4,128)}, u32[]{:S(2)}) copy-start(f32[3,1536]{1,0:T(4,128)} %get-tuple-element.10) | copy-start | bytes 55300
  285.3 22.8 %copy-start.3 = (f32[3,1536]{1,0:T(4,128)S(1)}, f32[3,1536]{1,0:T(4,128)}, u32[]{:S(2)}) copy-start(f32[3,1536]{1,0:T(4,128)} %get-tuple-element.8) | copy-start | bytes 55300
Sparse Core Ops, SparseCore 0:
  9.6 68.7 all-gather.4
  80.7 41.0 all-gather.6
  124.1 79.6 all-gather.10
  205.9 79.3 all-gather.8
where the time goes:
time: 320 us; the launch traced here: 318 us
  waiting for transfers between devices  243 us (76%)
  matrix products  35.8 us (11%)
  local copies, waits for them, and re-layouts  16.4 us (5%)
  between operations  13.3 us (4%)
  other arithmetic  6.74 us (2%)
    all_gather x1, waiting for transfers between devices, local(): full_up = lax.all_gather(w_up, 'win', axis=0, tiled=True)  81.5 us
    all_gather x1, waiting for transfers between devices, local(): full_down = lax.all_gather(w_down, 'win', axis=0, tiled=True)  77.9 us
    all_gather x1, waiting for transfers between devices, local(): full_qkv = lax.all_gather(w_qkv, 'win', axis=0, tiled=True)  47.8 us
    dot_general x1, matrix products, local(): jnp.dot(hidden, full_down, preferred_element_type=jnp.float32)  22.8 us
    all_gather x1, waiting for transfers between devices, local(): full_out = lax.all_gather(w_out, 'win', axis=0, tiled=True)  17.5 us
    ppermute x2, waiting for transfers between devices, passed_along(): lax.ppermute(shard, axis, [(i, (i + by) % length) for i in range(length)])  15.8 us
  transfers between devices with their start and end apart: 6, of which 6 were waited for; matrix products, arithmetic and copies ran while one was open for 10% of the time, Pallas kernels for 0%

commit v1 on v0

--- a/solution.py
+++ b/solution.py
@@ -1,6 +1,10 @@
+import functools
+
 import jax
 import jax.numpy as jnp
 from jax import lax
+from jax.experimental import pallas as pl
+from jax.experimental.pallas import tpu as pltpu
 from jax.sharding import PartitionSpec as P
 
 HEADS = 6
@@ -8,6 +12,170 @@
 WIN = 8
 LEVELS = 32
 
+MESH = pl.DeviceIdType.MESH
+SLOTS = 25
+
+
+class Gather:
+    def __init__(self, ring, shards, fulls, send, recv, local):
+        self.ring, self.shards, self.fulls = ring, shards, fulls
+        self.send, self.recv, self.local = send, recv, local
+        me = lax.axis_index("win")
+        self.c = lax.rem(me, 2)
+        self.y = lax.rem(me // 2, 2)
+        self.z = me // 4
+        self.g = lax.axis_index("groups")
+        self.h = lax.rem(self.g, 2)
+        up, down = lax.rem(self.z + 1, ring), lax.rem(self.z + ring - 1, ring)
+        self.across = lax.rem(self.z + 2, ring)
+        self.up, self.down = up, down
+        self.to_up = {"win": self.place(up, self.y, self.c)}
+        self.to_down = {"win": self.place(down, self.y, self.c)}
+        self.to_y = {"win": self.place(self.z, 1 - self.y, self.c)}
+        self.to_core = {"win": self.place(self.z, self.y, 1 - self.c)}
+        self.to_x = {"groups": self.g + 1 - 2 * self.h}
+        self.started = []
+
+    def place(self, z, y, c):
+        return (z * 2 + y) * 2 + c
+
+    def neighbours(self):
+        return [self.to_up, self.to_down, self.to_y, self.to_core, self.to_x]
+
+    def half(self, t, h):
+        width = self.shards[t].shape[1] // 2
+        return pl.ds(pl.multiple_of(h * width, 128), width)
+
+    def part(self, t, z, y, c, h=None):
+        depth = self.shards[t].shape[0]
+        rows = pl.ds(pl.multiple_of(self.place(z, y, c) * depth, depth), depth)
+        return self.fulls[t].at[rows] if h is None else self.fulls[t].at[rows, self.half(t, h)]
+
+    def copy(self, t, slot, src, dst, to):
+        at = t * SLOTS + slot
+        return pltpu.make_async_remote_copy(
+            src_ref=src,
+            dst_ref=dst,
+            send_sem=self.send.at[at],
+            recv_sem=self.recv.at[at],
+            device_id=to,
+            device_id_type=MESH,
+        )
+
+    def put(self, t, slot, src, dst, to):
+        made = self.copy(t, slot, src, dst, to)
+        made.start()
+        self.started.append(made)
+
+    def pass_on(self, t, slot, part, to):
+        self.put(t, slot, part, part, to)
+
+    def arrive(self, t, slot, part):
+        self.copy(t, slot, part, part, self.to_core).wait_recv()
+
+    def own(self, t):
+        shard = self.shards[t]
+        mine = self.part(t, self.z, self.y, self.c)
+        half = self.part(t, self.z, self.y, self.c, self.h)
+        self.put(t, 0, shard, mine, self.to_up)
+        self.put(t, 1, shard, mine, self.to_down)
+        self.put(t, 4, shard.at[:, self.half(t, self.h)], half, self.to_y)
+        self.put(t, 12, shard, mine, self.to_core)
+        pltpu.make_async_copy(shard, mine, self.local.at[t]).start()
+
+    def near(self, t):
+        for slot, z, half, to in ((0, self.down, 0, self.to_up), (1, self.up, 1, self.to_down)):
+            whole = self.part(t, z, self.y, self.c)
+            self.arrive(t, slot, whole)
+            self.pass_on(t, 2 + slot, self.part(t, z, self.y, self.c, half), to)
+            self.pass_on(t, 5 + slot, self.part(t, z, self.y, self.c, self.h), self.to_y)
+            self.pass_on(t, 13 + slot, whole, self.to_core)
+
+    def far(self, t):
+        for half in (0, 1):
+            part = self.part(t, self.across, self.y, self.c, half)
+            self.arrive(t, 2 + half, part)
+            self.pass_on(t, 15 + half, part, self.to_core)
+        self.pass_on(t, 7, self.part(t, self.across, self.y, self.c, self.h), self.to_y)
+
+    def turn(self, t, k):
+        z = (self.z, self.down, self.up, self.across)[k]
+        part = self.part(t, z, 1 - self.y, self.c, self.h)
+        self.arrive(t, 4 + k, part)
+        self.pass_on(t, 8 + k, part, self.to_x)
+        self.pass_on(t, 17 + k, part, self.to_core)
+
+    def last(self, t, k):
+        z = (self.z, self.down, self.up, self.across)[k]
+        part = self.part(t, z, 1 - self.y, self.c, 1 - self.h)
+        self.arrive(t, 8 + k, part)
+        self.pass_on(t, 21 + k, part, self.to_core)
+
+    def handed(self, t):
+        other = 1 - self.c
+        zs = (self.z, self.down, self.up, self.across)
+        mine = self.part(t, self.z, self.y, self.c)
+        pltpu.make_async_copy(self.shards[t], mine, self.local.at[t]).wait()
+        for k in range(3):
+            self.arrive(t, 12 + k, self.part(t, zs[k], self.y, other))
+        for half in (0, 1):
+            self.arrive(t, 15 + half, self.part(t, self.across, self.y, other, half))
+        for k in range(4):
+            self.arrive(t, 17 + k, self.part(t, zs[k], 1 - self.y, other, self.h))
+        for k in range(4):
+            self.arrive(t, 21 + k, self.part(t, zs[k], 1 - self.y, other, 1 - self.h))
+
+    def drain(self):
+        for made in self.started:
+            made.wait_send()
+
+
+def meet(neighbours):
+    barrier = pltpu.get_barrier_semaphore()
+    for to in neighbours:
+        pl.semaphore_signal(barrier, inc=1, device_id=to, device_id_type=MESH)
+    pl.semaphore_wait(barrier, len(neighbours))
+
+
+def gather_kernel(ring, *refs):
+    shards, fulls = refs[:4], refs[4:8]
+    gather = Gather(ring, shards, fulls, *refs[8:])
+    meet(gather.neighbours())
+    gather.own(0)
+    gather.own(1)
+    for t in range(4):
+        gather.near(t)
+        gather.turn(t, 0)
+        gather.far(t)
+        if t + 2 < 4:
+            gather.own(t + 2)
+        for k in (1, 2, 3):
+            gather.turn(t, k)
+        for k in range(4):
+            gather.last(t, k)
+    for t in range(4):
+        gather.handed(t)
+    gather.drain()
+
+
+def gather_all(shards):
+    count = lax.axis_size("win")
+    if count // 4 != 4 or lax.axis_size("groups") % 2:
+        return [lax.all_gather(shard, "win", axis=0, tiled=True) for shard in shards]
+    full = [jax.ShapeDtypeStruct((s.shape[0] * count, s.shape[1]), s.dtype) for s in shards]
+    return pl.pallas_call(
+        functools.partial(gather_kernel, count // 4),
+        out_shape=full,
+        in_specs=[pl.BlockSpec(memory_space=pltpu.VMEM)] * 4,
+        out_specs=[pl.BlockSpec(memory_space=pl.ANY)] * 4,
+        scratch_shapes=[
+            pltpu.SemaphoreType.DMA((4 * SLOTS,)),
+            pltpu.SemaphoreType.DMA((4 * SLOTS,)),
+            pltpu.SemaphoreType.DMA((4,)),
+        ],
+        compiler_params=pltpu.CompilerParams(collective_id=0, has_side_effects=True),
+    )(*shards)
+
 
 def passed_along(shard, axis, by):
     length = lax.axis_size(axis)
@@ -29,6 +197,7 @@
 
 def local(latents, offsets, levels, mod_table, rel_bias, w_qkv, w_out, w_up, w_down):
     batches, lat_rows, columns, features = latents.shape
+    full_qkv, full_out, full_up, full_down = gather_all((w_qkv, w_out, w_up, w_down))
     inner = HEADS * HEAD_DIM
     per_dev = columns // WIN
     selector = (levels[:, None] == jnp.arange(LEVELS, dtype=jnp.int32)[None, :]).astype(
@@ -45,7 +214,6 @@
     rolled = jax.vmap(
         lambda plane, shift_by: lax.dynamic_slice_in_dim(plane, WIN - shift_by, columns, 1)
     )(widened, offsets)
-    full_qkv = lax.all_gather(w_qkv, "win", axis=0, tiled=True)
     windows = rolled.reshape(batches, lat_rows, per_dev, WIN, features).transpose(0, 2, 1, 3, 4)
     windows = windows.reshape(-1, lat_rows * WIN, features)
     number = windows.shape[0]
@@ -61,7 +229,6 @@
     ).astype(jnp.bfloat16)
     attended = attended.reshape(batches, per_dev, lat_rows, WIN, inner).transpose(0, 2, 1, 3, 4)
     attended = attended.reshape(batches, lat_rows, columns, inner)
-    full_out = lax.all_gather(w_out, "win", axis=0, tiled=True)
     returned = passed_along(attended[:, :, :WIN, :], "win", -1)
     restored = restore_grid(attended, returned, offsets, columns)
     projected = jnp.dot(restored.reshape(-1, inner), full_out, preferred_element_type=jnp.float32)
@@ -70,10 +237,8 @@
     second = (
         norm_rows(middle.astype(jnp.float32)) * (1.0 + modulation[:, 3]) + modulation[:, 4]
     ).astype(jnp.bfloat16)
-    full_up = lax.all_gather(w_up, "win", axis=0, tiled=True)
     hidden = jnp.dot(second.reshape(-1, features), full_up, preferred_element_type=jnp.float32)
     hidden = jax.nn.gelu(hidden, approximate=False).astype(jnp.bfloat16)
-    full_down = lax.all_gather(w_down, "win", axis=0, tiled=True)
     lowered = jnp.dot(hidden, full_down, preferred_element_type=jnp.float32).reshape(
         batches, lat_rows, columns, features
     )

time: 320 us -> 242 us (0.76)
  waiting for transfers between devices: 243 us -> 7.04 us
  Pallas kernels: 0 us -> 171 us
  between operations: 13.3 us -> 0.23 us
    all_gather x4 -> x0, waiting for transfers between devices: 225 us -> none  [the longest x1 81.5 us: local(): full_up = lax.all_gather(w_up, 'win', axis=0, tiled=True)]
    pallas_call x0 -> x1, Pallas kernels: none -> 171 us  [gather_all(): pl.pallas_call(functools.partial(gather_kernel, count // 4), out_shape=fu...]
    ppermute x2, waiting for transfers between devices: 15.8 us -> 7.04 us  [passed_along(): lax.ppermute(shard, axis, [(i, (i + by) % length) for i in range(length)])]
  transfers between devices with their start and end apart: 6 -> 2, of which waited for: 6 -> 1; matrix products, arithmetic and copies ran while one was open for 10% -> 1% of each run, Pallas kernels for 0% -> 71%
where the time goes in v1:
time: 242 us; the launch traced here: 240 us
  Pallas kernels  171 us (71%)
  matrix products  35.4 us (15%)
  local copies, waits for them, and re-layouts  16.4 us (7%)
  other arithmetic  7.99 us (3%)
  waiting for transfers between devices  7.04 us (3%)
    pallas_call x1, Pallas kernels, gather_all(): pl.pallas_call(functools.partial(gather_kernel, count // 4), out_shape=fu...  171 us
    dot_general x1, matrix products, local(): jnp.dot(hidden, full_down, preferred_element_type=jnp.float32)  22.8 us
    ppermute x2, waiting for transfers between devices, passed_along(): lax.ppermute(shard, axis, [(i, (i + by) % length) for i in range(length)])  7.04 us
    dot_general x1, matrix products, local(): jnp.dot(windows.reshape(-1, features), full_qkv, preferred_element_type=j...  5.91 us
  transfers between devices with their start and end apart: 2, of which 1 were waited for; matrix products, arithmetic and copies ran while one was open for 1% of the time, Pallas kernels for 71%

profile of v1, /device:TPU:5, one launch (start us, length us, event | category | flops | bytes accessed | tf_op | source)
XLA Modules:
  0.0 240.4 jit_solution(16161440748115968742)
XLA Ops:
  0.0 1.1 copy-done
  1.1 0.9 convolution_bitcast_fusion
  2.0 0.7 slice_bitcast_fusion.1
  2.6 1.5 convert_reduce_fusion.1
  4.1 0.4 fusion.22
  4.6 0.7 fusion.25
  5.3 0.9 slice.55
  6.2 1.8 collective-permute-start
  8.0 1.7 copy.24
  9.7 171.2 %shard_map.91 = (bf16[1536,2304]{1,0:T(8,128)(2,1)}, bf16[768,1536]{1,0:T(8,128)(2,1)}, bf16[1536,3072]{1,0:T(8,128)(2,1)}, bf16[3072,1536]{1,0:T(8,128)(2,1)}) custom-call(bf16[96,2304]{1,0:T(8,128)(2,1)} %refs_0_.1, bf16[48,1536]{1,0:T(8,128)(2,1)} %refs_1_.1, bf16[96,3072]{1,0:T(8,128)(2,1)} %refs_2_.1, bf16[192,1536]{1,0:T(8,128)(2,1)} %refs_3_.1), custom_call_target="tpu_custom_call" | custom-call | tf_op jit(solution)/shard_map/pallas_call | solution.py:166
  180.9 0.1 pad_maximum_fusion
  181.1 0.5 copy.19
  181.6 1.7 gather_fusion
  183.2 1.6 copy.20
  184.9 5.9 %convolution_convert_fusion = bf16[384,2304]{1,0:T(8,128)(2,1)S(1)} fusion(bf16[384,1536]{1,0:T(8,128)(2,1)S(1)} %bitcast.93, bf16[1536,2304]{1,0:T(8,128)(2,1)} %get-tuple-element.9), kind=kOutput, calls=%fused_computation.22 | convolution fusion | flops 2718793728 | bytes 10027008 | tf_op jit(solution)/shard_map/dot_general | solution.py:220
  190.8 3.2 %reshape.85 = bf16[6,64,3,6,128]{4,3,2,1,0:T(8,128)(2,1)} reshape(bf16[384,2304]{1,0:T(8,128)(2,1)S(1)} %convolution_convert_fusion) | data formatting | bytes 3538944 | tf_op jit(solution)/shard_map/reshape | solution.py:221
  193.9 2.9 %fusion.109 = (bf16[6,64,1,6,128]{4,3,2,1,0:T(8,128)(2,1)S(1)}, bf16[6,64,1,6,128]{4,3,2,1,0:T(8,128)(2,1)}, bf16[6,64,1,6,128]{4,3,2,1,0:T(8,128)(2,1)S(1)}) fusion(bf16[6,64,3,6,128]{4,3,2,1,0:T(8,128)(2,1)} %reshape.85), kind=kLoop, calls=%fused_computation.150 | loop fusion | bytes 3538944 | tf_op jit(solution)/shard_map/slice | solution.py:223
  196.9 0.4 fusion.60
  197.3 0.3 fusion.110
  197.6 2.5 %fusion.61 = bf16[6,64,6,128]{3,1,2,0:T(8,128)(2,1)} fusion(bf16[6,64,1,6,128]{4,3,2,1,0:T(8,128)(2,1)} %get-tuple-element.14, f32[6,6,64]{2,1,0:T(8,128)S(1)} %fusion.110, f32[6,6,64,64]{2,3,1,0:T(8,128)S(1)} %fusion.60), kind=kOutput, calls=%fused_computation.83 | convolution fusion | flops 38488384 | bytes 1778688 | tf_op jit(solution)/shard_map/whqk,wkhe->wqhe/dot_general | solution.py:227
  200.1 1.5 copy.26
  201.6 0.7 reshape.86
  202.2 0.1 copy.27
  202.4 0.2 collective-permute-start.1
  202.6 7.0 %collective-permute-done.1 = bf16[3,8,8,768]{3,1,0,2:T(8,128)(2,1)S(1)} collective-permute-done((bf16[3,8,8,768]{3,1,0,2:T(8,128)(2,1)S(1)}, bf16[3,8,8,768]{3,1,0,2:T(8,128)(2,1)S(1)}, u32[]{:S(2)}, u32[]{:S(2)}) %collective-permute-start.1) | collective-permute-done | bytes 294944 | tf_op jit(solution)/shard_map/ppermute | solution.py:182
  209.7 0.1 pad_maximum_fusion.1
  209.7 0.6 gather_fusion.1
  210.4 2.9 %convert_reduce_fusion = (f32[3,8,16]{2,1,0:T(8,128)S(1)}, bf16[3,8,16,1536]{3,2,1,0:T(8,128)(2,1)S(1)}) fusion(bf16[768,1536]{1,0:T(8,128)(2,1)} %get-tuple-element.10, bf16[3,8,16,768]{3,1,2,0:T(8,128)(2,1)S(1)} %gather_fusion.1, f32[3,1536]{1,0:T(4,128)} %get-tuple-element.21, bf16[3,8,16,1536]{3,2,1,0:T(8,128)(2,1)S(1)} %copy-done.1), kind=kOutput, calls=%fused_computation.25 | convolution fusion | flops 909508224 | bytes 5328384 | tf_op jit(solution)/shard_map/dot_general | solution.py:234
  213.3 0.4 fusion.18
  213.7 0.7 fusion.21
  214.5 22.8 %fusion.16 = f32[384,1536]{1,0:T(8,128)} fusion(bf16[3072,1536]{1,0:T(8,128)(2,1)} %get-tuple-element.12, bf16[384,1536]{1,0:T(8,128)(2,1)S(1)} %bitcast.92, bf16[1536,3072]{1,0:T(8,128)(2,1)} %get-tuple-element.11), kind=kOutput, calls=%fused_computation.35 | convolution fusion | flops 7324434432 | bytes 22413312 | tf_op jit(solution)/shard_map/dot_general | solution.py:242
  237.3 3.1 %fusion.26 = bf16[3,8,16,1536]{3,2,1,0:T(8,128)(2,1)} fusion(bf16[3,8,16,1536]{3,2,1,0:T(8,128)(2,1)S(1)} %get-tuple-element.25, f32[3,8,16,1536]{3,2,1,0:T(8,128)} %bitcast.90, f32[3,1536]{1,0:T(4,128)S(1)} %copy-done.3), kind=kLoop, calls=%fused_computation.44 | loop fusion | flops 2359296 | bytes 4737024 | tf_op jit(solution)/shard_map/convert_element_type | solution.py:245
  (20 shorter events, 0.1 us)
Async XLA Ops:
  0.0 1.1 copy-start
  0.0 4.1 %copy-start.1 = (bf16[3,8,16,1536]{3,2,1,0:T(8,128)(2,1)S(1)}, bf16[3,8,16,1536]{3,2,1,0:T(8,128)(2,1)}, u32[]{:S(2)}) copy-start(bf16[3,8,16,1536]{3,2,1,0:T(8,128)(2,1)} %param.9) | copy-start | bytes 3538948
  4.6 176.3 %copy-start.6 = (s32[3]{0:T(128)S(1)}, s32[3]{0:T(128)}, u32[]{:S(2)}) copy-start(s32[3]{0:T(128)} %param.10) | copy-start | bytes 40
  6.2 174.8 %collective-permute-start = (bf16[3,8,8,1536]{3,2,1,0:T(8,128)(2,1)}, bf16[3,8,8,1536]{3,2,1,0:T(8,128)(2,1)S(1)}, u32[]{:S(2)}, u32[]{:S(2)}) collective-permute-start(bf16[3,8,8,1536]{3,2,1,0:T(8,128)(2,1)} %slice.55), channel_id=1, source_target_pairs={{0,1},{1,2},{2,3},{3,4},{4,5},{5,6},{6,7},{7,8},{8,9},{9,10},{10,1... | collective-permute-start | bytes 1769480 | tf_op jit(solution)/shard_map/ppermute | solution.py:182
  193.9 2.9 %copy-start.2 = (f32[6,64,64]{1,2,0:T(8,128)S(1)}, f32[6,64,64]{1,2,0:T(8,128)}, u32[]{:S(2)}) copy-start(f32[6,64,64]{1,2,0:T(8,128)} %copy.24) | copy-start | bytes 294916
  202.4 7.3 %collective-permute-start.1 = (bf16[3,8,8,768]{3,1,0,2:T(8,128)(2,1)S(1)}, bf16[3,8,8,768]{3,1,0,2:T(8,128)(2,1)S(1)}, u32[]{:S(2)}, u32[]{:S(2)}) collective-permute-start(bf16[3,8,8,768]{3,1,0,2:T(8,128)(2,1)S(1)} %slice.59), channel_id=1, source_target_pairs={{0,15},{1,0},{2,1},{3,2},{4,3},{5,4},{6,5},{7,6},{8,7},{9,8},{10,9... | collective-permute-start | bytes 884744 | tf_op jit(solution)/shard_map/ppermute | solution.py:182
  210.3 3.4 %copy-start.4 = (f32[3,1536]{1,0:T(4,128)S(1)}, f32[3,1536]{1,0:T(4,128)}, u32[]{:S(2)}) copy-start(f32[3,1536]{1,0:T(4,128)} %get-tuple-element.17) | copy-start | bytes 55300
  210.4 3.4 %copy-start.5 = (f32[3,1536]{1,0:T(4,128)S(1)}, f32[3,1536]{1,0:T(4,128)}, u32[]{:S(2)}) copy-start(f32[3,1536]{1,0:T(4,128)} %get-tuple-element.18) | copy-start | bytes 55300
  214.4 22.9 %copy-start.3 = (f32[3,1536]{1,0:T(4,128)S(1)}, f32[3,1536]{1,0:T(4,128)}, u32[]{:S(2)}) copy-start(f32[3,1536]{1,0:T(4,128)} %get-tuple-element.16) | copy-start | bytes 55300

commit v2 on v0

--- a/solution.py
+++ b/solution.py
@@ -1,6 +1,10 @@
+import functools
+
 import jax
 import jax.numpy as jnp
 from jax import lax
+from jax.experimental import pallas as pl
+from jax.experimental.pallas import tpu as pltpu
 from jax.sharding import PartitionSpec as P
 
 HEADS = 6
@@ -8,6 +12,174 @@
 WIN = 8
 LEVELS = 32
 
+MESH = pl.DeviceIdType.MESH
+SLOTS = 28
+LINE = 4
+UP, DOWN, ALONG_Y, ALONG_X, FAR_X, HAND, HAND_FAR, HAND_Y, HAND_X = 0, 3, 6, 10, 14, 15, 19, 20, 24
+
+ORDER = (
+    (1, 1), (0, 2), (1, 2), (0, 3), (3, 0), (2, 1), (1, 3), (0, 4), (0, 5), (1, 4), (1, 5), (2, 2),
+    (2, 3), (3, 1), (2, 4), (3, 2), (2, 5), (3, 3), (3, 4), (3, 5),
+)
+
+
+def under(condition, act):
+    if condition is None:
+        act()
+    else:
+        pl.when(condition)(act)
+
+
+class Gather:
+    def __init__(self, shards, fulls, send, recv, local):
+        self.shards, self.fulls = shards, fulls
+        self.send, self.recv, self.local = send, recv, local
+        me = lax.axis_index("win")
+        self.c = lax.rem(me, 2)
+        self.y = lax.rem(me // 2, 2)
+        self.z = me // 4
+        self.g = lax.axis_index("groups")
+        self.h = lax.rem(self.g, 2)
+        up, down = lax.rem(self.z + 1, LINE), lax.rem(self.z + LINE - 1, LINE)
+        self.to_up = {"win": self.place(up, self.y, self.c)}
+        self.to_down = {"win": self.place(down, self.y, self.c)}
+        self.to_y = {"win": self.place(self.z, 1 - self.y, self.c)}
+        self.to_core = {"win": self.place(self.z, self.y, 1 - self.c)}
+        self.to_x = {"groups": self.g + 1 - 2 * self.h}
+        self.started = []
+
+    def place(self, z, y, c):
+        return (z * 2 + y) * 2 + c
+
+    def neighbours(self):
+        return [self.to_up, self.to_down, self.to_y, self.to_core, self.to_x]
+
+    def half(self, t, h):
+        width = self.shards[t].shape[1] // 2
+        return pl.ds(pl.multiple_of(h * width, 128), width)
+
+    def part(self, t, z, y, c, h=None):
+        depth = self.shards[t].shape[0]
+        rows = pl.ds(pl.multiple_of(self.place(z, y, c) * depth, depth), depth)
+        return self.fulls[t].at[rows] if h is None else self.fulls[t].at[rows, self.half(t, h)]
+
+    def copy(self, t, slot, src, dst, to):
+        at = t * SLOTS + slot
+        return pltpu.make_async_remote_copy(
+            src_ref=src,
+            dst_ref=dst,
+            send_sem=self.send.at[at],
+            recv_sem=self.recv.at[at],
+            device_id=to,
+            device_id_type=MESH,
+        )
+
+    def put(self, condition, make):
+        under(condition, lambda: make().start())
+        self.started.append((condition, make))
+
+    def pass_on(self, condition, t, slot, part, to):
+        self.put(condition, lambda: self.copy(t, slot, part(), part(), to))
+
+    def arrive(self, condition, t, slot, part):
+        under(condition, lambda: self.copy(t, slot, part(), part(), self.to_core).wait_recv())
+
+    def mine(self, t, z, h=None):
+        return lambda: self.part(t, z, self.y, self.c, h)
+
+    def own(self, t):
+        shard = self.shards[t]
+        mine, half = self.mine(t, self.z), self.mine(t, self.z, self.h)
+        up, down = self.z + 1 < LINE, self.z >= 1
+        self.put(up, lambda: self.copy(t, UP, shard, mine(), self.to_up))
+        self.put(down, lambda: self.copy(t, DOWN, shard, mine(), self.to_down))
+        source = shard.at[:, self.half(t, self.h)]
+        self.put(None, lambda: self.copy(t, ALONG_Y + self.z, source, half(), self.to_y))
+        self.put(None, lambda: self.copy(t, HAND + self.z, shard, mine(), self.to_core))
+        pltpu.make_async_copy(shard, mine(), self.local.at[t]).start()
+
+    def sources(self, d):
+        return ((self.z >= d, self.z - d), (self.z + d < LINE, self.z + d))
+
+    def come(self, t, d):
+        ways = ((UP, self.z + 1 < LINE, self.to_up), (DOWN, self.z >= 1, self.to_down))
+        h = self.h if d == 3 else None
+        for (there, z), (way, more, to) in zip(self.sources(d), ways):
+            part = self.mine(t, z, h)
+            self.arrive(there, t, way + d - 1, part)
+            if d < 3:
+                onward = self.mine(t, z, self.h if d == 2 else None)
+                self.pass_on(there & more, t, way + d, onward, to)
+            self.pass_on(there, t, ALONG_Y + z, self.mine(t, z, self.h), self.to_y)
+            if d == 3:
+                self.pass_on(there, t, FAR_X, part, self.to_x)
+            self.pass_on(there, t, HAND + z, part, self.to_core)
+
+    def at(self, d):
+        return ((None, self.z),) if d == 0 else self.sources(d)
+
+    def turn(self, t, d):
+        for there, z in self.at(d):
+            part = lambda z=z: self.part(t, z, 1 - self.y, self.c, self.h)
+            self.arrive(there, t, ALONG_Y + z, part)
+            self.pass_on(there, t, ALONG_X + z, part, self.to_x)
+            self.pass_on(there, t, HAND_Y + z, part, self.to_core)
+
+    def last(self, t, d):
+        for there, z in self.at(d):
+            part = lambda z=z: self.part(t, z, 1 - self.y, self.c, 1 - self.h)
+            self.arrive(there, t, ALONG_X + z, part)
+            self.pass_on(there, t, HAND_X + z, part, self.to_core)
+
+    def other(self, t):
+        for there, z in self.sources(3):
+            part = self.mine(t, z, 1 - self.h)
+            self.arrive(there, t, FAR_X, part)
+            self.pass_on(there, t, HAND_FAR, part, self.to_core)
+
+    def handed(self, t):
+        core = 1 - self.c
+        pltpu.make_async_copy(self.shards[t], self.mine(t, self.z)(), self.local.at[t]).wait()
+        for d in range(LINE):
+            for there, z in self.at(d):
+                for slot, y, h in (
+                    (HAND + z, self.y, self.h if d == 3 else None),
+                    (HAND_Y + z, 1 - self.y, self.h),
+                    (HAND_X + z, 1 - self.y, 1 - self.h),
+                ):
+                    part = lambda z=z, y=y, h=h: self.part(t, z, y, core, h)
+                    self.arrive(there, t, slot, part)
+        for there, z in self.sources(3):
+            part = lambda z=z: self.part(t, z, self.y, core, 1 - self.h)
+            self.arrive(there, t, HAND_FAR, part)
+
+    def stage(self, t, number):
+        if number == 0:
+            return [lambda: self.own(t)]
+        events = []
+        if number <= 3:
+            events.append(lambda: self.come(t, number))
+        if number == 4:
+            events.append(lambda: self.other(t))
+        if 1 <= number <= 4:
+            events.append(lambda: self.turn(t, number - 1))
+        if 2 <= number <= 5:
+            events.append(lambda: self.last(t, number - 2))
+        if number == 5:
+            events.append(lambda: self.handed(t))
+        return events
+
+    def drain(self):
+        for condition, make in self.started:
+            under(condition, lambda make=make: make().wait_send())
+
+
+def meet(neighbours):
+    barrier = pltpu.get_barrier_semaphore()
+    for to in neighbours:
+        pl.semaphore_signal(barrier, inc=1, device_id=to, device_id_type=MESH)
+    pl.semaphore_wait(barrier, len(neighbours))
+
 
 def passed_along(shard, axis, by):
     length = lax.axis_size(axis)
@@ -27,7 +199,7 @@
     )
 
 
-def local(latents, offsets, levels, mod_table, rel_bias, w_qkv, w_out, w_up, w_down):
+def plain(latents, offsets, levels, mod_table, rel_bias, w_qkv, w_out, w_up, w_down):
     batches, lat_rows, columns, features = latents.shape
     inner = HEADS * HEAD_DIM
     per_dev = columns // WIN
@@ -80,6 +252,247 @@
     return (middle.astype(jnp.float32) + modulation[:, 5] * lowered).astype(jnp.bfloat16)
 
 
+def spread(work, events):
+    done = 0
+    for index, piece in enumerate(work):
+        piece()
+        upto = (len(events) * (index + 1)) // len(work)
+        for event in events[done:upto]:
+            event()
+        done = upto
+
+
+def pieces(count, step, act):
+    def piece(first):
+        lax.fori_loop(first, min(first + step, count), lambda i, _: (act(i), 0)[1], 0)
+
+    return [functools.partial(piece, first) for first in range(0, count, step)]
+
+
+def kernel(
+    batches, block, area, lat_ref, low_ref, high_ref, mod_ref, gather_in_ref, gather_out_ref,
+    bias_ref, s0, s1, s2, s3, out_ref, f0, f1, f2, f3, prev, after, normed, wins, triple, heads,
+    restored, middle, second, hidden, send, recv, local, halo_send, halo_recv,
+):
+    features = lat_ref.shape[1]
+    inner = HEADS * HEAD_DIM
+    own = lat_ref.shape[0] // batches
+    side = low_ref.shape[0] // batches
+    wide = own + 2 * side
+    moved = wins.shape[0] // batches
+    gather = Gather((s0, s1, s2, s3), (f0, f1, f2, f3), send, recv, local)
+    me, count = lax.axis_index("win"), lax.axis_size("win")
+    right, left = {"win": lax.rem(me + 1, count)}, {"win": lax.rem(me + count - 1, count)}
+    meet(gather.neighbours() + [right, left])
+    halos = []
+    for at, src, dst, to in ((0, high_ref, prev, right), (1, low_ref, after, left)):
+        made = pltpu.make_async_remote_copy(
+            src_ref=src,
+            dst_ref=dst,
+            send_sem=halo_send.at[at],
+            recv_sem=halo_recv.at[at],
+            device_id=to,
+            device_id_type=MESH,
+        )
+        made.start()
+        halos.append(made)
+    gather.own(0)
+    gather.own(1)
+
+    def norm_into(src, first, dst, start, m, scale, shift):
+        rows = src[pl.ds(first, block), :].astype(jnp.float32)
+        value = norm_rows(rows) * (1.0 + mod_ref[m, pl.ds(scale, 1), :])
+        value = value + mod_ref[m, pl.ds(shift, 1), :]
+        dst[pl.ds(start, block), :] = value.astype(jnp.bfloat16)
+
+    for m in range(batches):
+        def norm_own(i, _):
+            norm_into(lat_ref, m * own + i * block, normed, m * wide + side + i * block, m, 0, 1)
+            return 0
+
+        lax.fori_loop(0, own // block, norm_own, 0)
+    gather.come(0, 1)
+    for made in halos:
+        made.wait()
+    for m in range(batches):
+        for src, base in ((prev, 0), (after, side + own)):
+            def norm_side(i, _):
+                norm_into(src, m * side + i * block, normed, m * wide + base + i * block, m, 0, 1)
+                return 0
+
+            lax.fori_loop(0, side // block, norm_side, 0)
+    gather.turn(0, 0)
+    gather.own(2)
+
+    def arrange(m):
+        rows = normed[pl.ds(pl.multiple_of(m * wide, 16), wide), :]
+        wins[pl.ds(pl.multiple_of(m * moved, 16), moved), :] = jnp.dot(
+            gather_in_ref[m], rows, preferred_element_type=jnp.float32
+        ).astype(jnp.bfloat16)
+
+    width = 256
+
+    def columns(i):
+        return pl.ds(pl.multiple_of(i * width, width), width)
+
+    def project(i):
+        triple[:, columns(i)] = jnp.dot(
+            wins[...], f0[:, columns(i)], preferred_element_type=jnp.float32
+        ).astype(jnp.bfloat16)
+
+    def attend(w):
+        rows = pl.ds(pl.multiple_of(w * area, area), area)
+        for head in range(HEADS):
+            def of(which):
+                return triple[rows, pl.ds(which * inner + head * HEAD_DIM, HEAD_DIM)]
+
+            scores = lax.dot_general(
+                of(0), of(1), (((1,), (1,)), ((), ())), preferred_element_type=jnp.float32
+            )
+            scores = scores * (1.0 / HEAD_DIM**0.5) + bias_ref[head]
+            powers = jnp.exp(scores - jnp.max(scores, axis=-1, keepdims=True))
+            probs = (powers / jnp.sum(powers, axis=-1, keepdims=True)).astype(jnp.bfloat16)
+            heads[rows, pl.ds(head * HEAD_DIM, HEAD_DIM)] = jnp.dot(
+                probs, of(2), preferred_element_type=jnp.float32
+            ).astype(jnp.bfloat16)
+
+    def restore(m):
+        rows = heads[pl.ds(pl.multiple_of(m * moved, 16), moved), :]
+        restored[pl.ds(pl.multiple_of(m * own, 16), own), :] = jnp.dot(
+            gather_out_ref[m], rows, preferred_element_type=jnp.float32
+        ).astype(jnp.bfloat16)
+
+    def add(base_ref, dst, found, which, i):
+        for m in range(batches):
+            rows = pl.ds(m * own, own)
+            change = mod_ref[m, pl.ds(which, 1), columns(i)] * found[m * own : (m + 1) * own]
+            dst[rows, columns(i)] = (
+                base_ref[rows, columns(i)].astype(jnp.float32) + change
+            ).astype(jnp.bfloat16)
+
+    def settle(i):
+        found = jnp.dot(restored[...], f1[:, columns(i)], preferred_element_type=jnp.float32)
+        add(lat_ref, middle, found, 2, i)
+
+    def lift(i):
+        found = jnp.dot(second[...], f2[:, columns(i)], preferred_element_type=jnp.float32)
+        found = 0.5 * found * (1.0 + lax.erf(found * (0.5**0.5)))
+        hidden[:, columns(i)] = found.astype(jnp.bfloat16)
+
+    def lower(i):
+        found = jnp.dot(hidden[...], f3[:, columns(i)], preferred_element_type=jnp.float32)
+        add(middle, out_ref, found, 5, i)
+
+    for m in range(batches):
+        arrange(m)
+    lined = [(t, event) for t, number in ORDER for event in gather.stage(t, number)]
+    index = max(i for i, (t, _) in enumerate(lined) if t == 0) + 1
+    for _, event in lined[:index]:
+        event()
+    lined = lined[index:]
+    index = max(i for i, (t, _) in enumerate(lined) if t == 1) + 1
+    work = pieces(triple.shape[1] // width, 3, project) + pieces(wins.shape[0] // area, 2, attend)
+    spread(work, [event for _, event in lined[:index]])
+    lined = lined[index:]
+    for m in range(batches):
+        restore(m)
+    index = max(i for i, (t, _) in enumerate(lined) if t == 2) + 1
+    work = pieces(features // width, 3, settle)
+    spread(work, [])
+    for m in range(batches):
+        def norm_again(i, _):
+            at = m * own + i * block
+            norm_into(middle, at, second, at, m, 3, 4)
+            return 0
+
+        lax.fori_loop(0, own // block, norm_again, 0)
+    for _, event in lined[:index]:
+        event()
+    lined = lined[index:]
+    spread(pieces(hidden.shape[1] // width, 2, lift), [event for _, event in lined])
+    spread(pieces(features // width, features // width, lower), [])
+    gather.drain()
+
+
+def local(latents, offsets, levels, mod_table, rel_bias, w_qkv, w_out, w_up, w_down):
+    count = lax.axis_size("win")
+    batches, lat_rows, columns, features = latents.shape
+    if count != 4 * LINE or lax.axis_size("groups") % 2 or columns < WIN:
+        return plain(
+            latents, offsets, levels, mod_table, rel_bias, w_qkv, w_out, w_up, w_down
+        )
+    selector = (levels[:, None] == jnp.arange(LEVELS, dtype=jnp.int32)[None, :]).astype(
+        jnp.bfloat16
+    )
+    modulation = jnp.dot(
+        selector, mod_table.reshape(LEVELS, 6 * features), preferred_element_type=jnp.float32
+    ).reshape(batches, 6, features)
+    area = lat_rows * WIN
+    bands = columns // WIN + 1
+    own, moved = lat_rows * columns, bands * area
+    row = jnp.arange(lat_rows, dtype=jnp.int32)
+
+    def spots(first, size):
+        place = first + jnp.arange(size, dtype=jnp.int32)
+        both = jnp.broadcast_to(row[:, None], (lat_rows, size)), jnp.broadcast_to(
+            place[None], (lat_rows, size)
+        )
+        return [part.reshape(-1) for part in both]
+
+    def joined(parts):
+        return [jnp.concatenate(side) for side in zip(*parts)]
+
+    wide_row, wide_at = joined(
+        [spots(0, WIN), spots(WIN, columns), spots(WIN + columns, WIN)]
+    )
+    rolled_row, rolled_at = joined([spots(band * WIN, WIN) for band in range(bands)])
+    own_row, own_at = spots(0, columns)
+    by = offsets[:, None, None]
+    gather_in = (rolled_row[:, None] == wide_row[None]) & (
+        rolled_at[None, :, None] + WIN - by == wide_at[None, None]
+    )
+    gather_out = (own_row[:, None] == rolled_row[None]) & (
+        own_at[None, :, None] + by == rolled_at[None, None]
+    )
+    low = latents[:, :, :WIN].reshape(-1, features)
+    high = latents[:, :, columns - WIN :].reshape(-1, features)
+    shards = (w_qkv, w_out, w_up, w_down)
+    vmem = pl.BlockSpec(memory_space=pltpu.VMEM)
+    total = batches * own
+    bf = jnp.bfloat16
+    found = pl.pallas_call(
+        functools.partial(kernel, batches, 32, area),
+        out_shape=jax.ShapeDtypeStruct((total, features), bf),
+        in_specs=[vmem] * 11,
+        out_specs=vmem,
+        scratch_shapes=[pltpu.VMEM((s.shape[0] * count, s.shape[1]), bf) for s in shards]
+        + [
+            pltpu.VMEM(low.shape, bf),
+            pltpu.VMEM(low.shape, bf),
+            pltpu.VMEM((batches * (own + 2 * area), features), bf),
+            pltpu.VMEM((batches * moved, features), bf),
+            pltpu.VMEM((batches * moved, w_qkv.shape[1]), bf),
+            pltpu.VMEM((batches * moved, w_out.shape[0] * count), bf),
+            pltpu.VMEM((total, w_out.shape[0] * count), bf),
+            pltpu.VMEM((total, features), bf),
+            pltpu.VMEM((total, features), bf),
+            pltpu.VMEM((total, w_up.shape[1]), bf),
+            pltpu.SemaphoreType.DMA((4 * SLOTS,)),
+            pltpu.SemaphoreType.DMA((4 * SLOTS,)),
+            pltpu.SemaphoreType.DMA((4,)),
+            pltpu.SemaphoreType.DMA((2,)),
+            pltpu.SemaphoreType.DMA((2,)),
+        ],
+        compiler_params=pltpu.CompilerParams(
+            collective_id=0, has_side_effects=True, vmem_limit_bytes=62 * 2**20
+        ),
+    )(
+        latents.reshape(total, features), low, high, modulation, gather_in.astype(bf),
+        gather_out.astype(bf), rel_bias, *shards,
+    )
+    return found.reshape(latents.shape)
+
+
 def solution(mesh):
     in_specs = (
         P("groups", None, "win", None),

time: 320 us -> 188 us (0.59)
  waiting for transfers between devices: 243 us -> 0 us
  Pallas kernels: 0 us -> 178 us
  matrix products: 35.8 us -> 0.91 us
  between operations: 13.3 us -> 0.08 us
  local copies, waits for them, and re-layouts: 16.4 us -> 4.88 us
    all_gather x4 -> x0, waiting for transfers between devices: 225 us -> none  [the longest x1 81.5 us: local(): full_up = lax.all_gather(w_up, 'win', axis=0, tiled=True)]
    pallas_call x0 -> x1, Pallas kernels: none -> 178 us  [local(): pl.pallas_call(functools.partial(kernel, batches, 32, area), out_shape=ja...]
    dot_general x5 -> x0, matrix products: 34.9 us -> none  [the longest x1 22.8 us: local(): jnp.dot(hidden, full_down, preferred_element_type=jnp.float32)]
    ppermute x2 -> x0, waiting for transfers between devices: 15.8 us -> none  [passed_along(): lax.ppermute(shard, axis, [(i, (i + by) % length) for i in range(length)])]
    reshape x3 -> x4, local copies, waits for them, and re-layouts: 6.49 us -> 0.32 us  [spots(): return [part.reshape(-1) for part in both]]
  transfers between devices with their start and end apart: 6 -> 0, of which waited for: 6 -> 0; matrix products, arithmetic and copies ran while one was open for 10% -> 0% of each run, Pallas kernels for 0% -> 0%
where the time goes in v2:
time: 188 us
  Pallas kernels  178 us (95%)
  local copies, waits for them, and re-layouts  4.88 us (3%)
  other arithmetic  3.72 us (2%)
    pallas_call x1, Pallas kernels, local(): pl.pallas_call(functools.partial(kernel, batches, 32, area), out_shape=ja...  178 us

profile of v2, /device:TPU:5, one launch (start us, length us, event | category | flops | bytes accessed | tf_op | source)
XLA Modules:
  0.0 187.8 jit_solution(11530453604857758524)
XLA Ops:
  0.0 0.0 copy-start
  0.0 0.0 copy-start.1
  0.1 0.1 reshape.223
  0.1 0.1 reshape.222
  0.2 0.1 concatenate.28
  0.3 0.1 concatenate.27
  0.4 0.1 add.65
  0.5 0.8 broadcast_add_fusion
  1.3 0.1 concatenate.26
  1.3 0.1 pad_add_fusion.3
  1.4 0.1 broadcast_add_fusion.1
  1.5 0.7 broadcast_subtract_fusion
  2.2 0.1 reshape.221
  2.3 0.1 reshape.220
  2.4 0.1 pad_add_fusion
  2.5 0.1 pad_add_fusion.1
  2.6 0.1 broadcast_compare_fusion.1
  2.7 0.1 broadcast_compare_fusion
  2.8 0.0 copy-done
  2.8 0.9 fusion
  3.7 0.7 copy.13.mod_ref
  4.4 0.8 and_convert_fusion.1.gather_out_ref
  5.2 0.9 and_convert_fusion.gather_in_ref
  6.1 0.0 copy-done.1
  6.1 1.1 fusion.6
  7.2 178.2 %shard_map.91 = bf16[384,1536]{1,0:T(8,128)(2,1)} custom-call(bf16[384,1536]{1,0:T(8,128)(2,1)} %bitcast.22, bf16[192,1536]{1,0:T(8,128)(2,1)} %bitcast.25, bf16[192,1536]{1,0:T(8,128)(2,1)} %bitcast.24, f32[3,6,1536]{2,1,0:T(8,128)} %copy.13.mod_ref, bf16[3,192,256]{2,1,0:T(8,128)(2,1)} %and_convert_fusion.gather_in_ref, ...), custom_call_target="tpu_custom_call" | custom-call | tf_op jit(solution)/shard_map/pallas_call | solution.py:463
  185.4 2.4 %copy.24 = bf16[3,8,16,1536]{3,2,1,0:T(8,128)(2,1)} copy(bf16[3,8,16,1536]{3,2,1,0:T(8,128)(2,1)} %bitcast.23) | data formatting | bytes 2359296
  (12 shorter events, 0.0 us)
Async XLA Ops:
  0.0 2.8 %copy-start = (bf16[32,6,1536]{2,0,1:T(8,128)(2,1)S(1)}, bf16[32,6,1536]{2,0,1:T(8,128)(2,1)}, u32[]{:S(2)}) copy-start(bf16[32,6,1536]{2,0,1:T(8,128)(2,1)} %param.12) | copy-start | bytes 1769476
  0.0 6.1 %copy-start.1 = (bf16[3,8,16,1536]{3,2,1,0:T(8,128)(2,1)S(1)}, bf16[3,8,16,1536]{3,2,1,0:T(8,128)(2,1)}, u32[]{:S(2)}) copy-start(bf16[3,8,16,1536]{3,2,1,0:T(8,128)(2,1)} %param.9) | copy-start | bytes 3538948

commit v3 on v2

--- a/solution.py
+++ b/solution.py
@@ -17,9 +17,17 @@
 LINE = 4
 UP, DOWN, ALONG_Y, ALONG_X, FAR_X, HAND, HAND_FAR, HAND_Y, HAND_X = 0, 3, 6, 10, 14, 15, 19, 20, 24
 
+OWN, COME, TURN, LAST, OTHER = range(5)
 ORDER = (
-    (1, 1), (0, 2), (1, 2), (0, 3), (3, 0), (2, 1), (1, 3), (0, 4), (0, 5), (1, 4), (1, 5), (2, 2),
-    (2, 3), (3, 1), (2, 4), (3, 2), (2, 5), (3, 3), (3, 4), (3, 5),
+    (TURN, 0, 0), (TURN, 1, 0), (COME, 0, 1), (COME, 1, 1), (TURN, 0, 1), (COME, 0, 2),
+    (COME, 1, 2), (TURN, 1, 1), (OWN, 2, 0), (LAST, 0, 0), (TURN, 0, 2), (COME, 1, 3),
+    (COME, 0, 3), (TURN, 1, 2), (TURN, 1, 3), (LAST, 1, 3), (COME, 2, 1), (TURN, 0, 3),
+    (LAST, 1, 0), (TURN, 2, 0), (OTHER, 1, 0), (TURN, 2, 1), (LAST, 1, 2), (OWN, 3, 0),
+    (TURN, 3, 0), (OTHER, 0, 0), (LAST, 1, 1), (COME, 2, 2), (LAST, 0, 3), (LAST, 0, 1),
+    (LAST, 0, 2), (LAST, 2, 0), (COME, 3, 1), (TURN, 2, 2), (COME, 2, 3), (TURN, 3, 1),
+    (COME, 3, 2), (OTHER, 2, 0), (TURN, 2, 3), (LAST, 2, 1), (COME, 3, 3), (LAST, 2, 3),
+    (LAST, 2, 2), (TURN, 3, 2), (LAST, 3, 1), (LAST, 3, 0), (TURN, 3, 3), (LAST, 3, 2),
+    (OTHER, 3, 0), (LAST, 3, 3),
 )
 
 
@@ -153,21 +161,13 @@
             part = lambda z=z: self.part(t, z, self.y, core, 1 - self.h)
             self.arrive(there, t, HAND_FAR, part)
 
-    def stage(self, t, number):
-        if number == 0:
-            return [lambda: self.own(t)]
-        events = []
-        if number <= 3:
-            events.append(lambda: self.come(t, number))
-        if number == 4:
-            events.append(lambda: self.other(t))
-        if 1 <= number <= 4:
-            events.append(lambda: self.turn(t, number - 1))
-        if 2 <= number <= 5:
-            events.append(lambda: self.last(t, number - 2))
-        if number == 5:
-            events.append(lambda: self.handed(t))
-        return events
+    def event(self, kind, t, d):
+        if kind == OWN:
+            self.own(t)
+        elif kind == OTHER:
+            self.other(t)
+        else:
+            {COME: self.come, TURN: self.turn, LAST: self.last}[kind](t, d)
 
     def drain(self):
         for condition, make in self.started:
@@ -305,24 +305,17 @@
         value = value + mod_ref[m, pl.ds(shift, 1), :]
         dst[pl.ds(start, block), :] = value.astype(jnp.bfloat16)
 
-    for m in range(batches):
-        def norm_own(i, _):
+    def norm_own(i):
+        for m in range(batches):
             norm_into(lat_ref, m * own + i * block, normed, m * wide + side + i * block, m, 0, 1)
-            return 0
-
-        lax.fori_loop(0, own // block, norm_own, 0)
-    gather.come(0, 1)
-    for made in halos:
-        made.wait()
-    for m in range(batches):
-        for src, base in ((prev, 0), (after, side + own)):
-            def norm_side(i, _):
+
+    def norm_side(i):
+        if i == 0:
+            for made in halos:
+                made.wait()
+        for m in range(batches):
+            for src, base in ((prev, 0), (after, side + own)):
                 norm_into(src, m * side + i * block, normed, m * wide + base + i * block, m, 0, 1)
-                return 0
-
-            lax.fori_loop(0, side // block, norm_side, 0)
-    gather.turn(0, 0)
-    gather.own(2)
 
     def arrange(m):
         rows = normed[pl.ds(pl.multiple_of(m * wide, 16), wide), :]
@@ -383,33 +376,39 @@
         found = jnp.dot(hidden[...], f3[:, columns(i)], preferred_element_type=jnp.float32)
         add(middle, out_ref, found, 5, i)
 
-    for m in range(batches):
-        arrange(m)
-    lined = [(t, event) for t, number in ORDER for event in gather.stage(t, number)]
-    index = max(i for i, (t, _) in enumerate(lined) if t == 0) + 1
-    for _, event in lined[:index]:
-        event()
-    lined = lined[index:]
-    index = max(i for i, (t, _) in enumerate(lined) if t == 1) + 1
-    work = pieces(triple.shape[1] // width, 3, project) + pieces(wins.shape[0] // area, 2, attend)
-    spread(work, [event for _, event in lined[:index]])
-    lined = lined[index:]
-    for m in range(batches):
-        restore(m)
-    index = max(i for i, (t, _) in enumerate(lined) if t == 2) + 1
-    work = pieces(features // width, 3, settle)
-    spread(work, [])
-    for m in range(batches):
-        def norm_again(i, _):
+    def norm_again(i):
+        for m in range(batches):
             at = m * own + i * block
             norm_into(middle, at, second, at, m, 3, 4)
-            return 0
-
-        lax.fori_loop(0, own // block, norm_again, 0)
-    for _, event in lined[:index]:
+
+    events = [(t, functools.partial(gather.event, kind, t, d)) for kind, t, d in ORDER]
+
+    def until(*ts):
+        index = max([i for i, (t, _) in enumerate(events) if t in ts], default=-1) + 1
+        taken = [event for _, event in events[:index]]
+        del events[:index]
+        return taken
+
+    def each(act, count):
+        return [functools.partial(act, i) for i in range(count)]
+
+    def restore_all():
+        for m in range(batches):
+            restore(m)
+        gather.handed(1)
+
+    first = each(norm_own, own // block) + each(norm_side, side // block) + each(arrange, batches)
+    early = until(0)
+    spread(first, early[: len(first) + 3])
+    for event in early[len(first) + 3 :]:
         event()
-    lined = lined[index:]
-    spread(pieces(hidden.shape[1] // width, 2, lift), [event for _, event in lined])
+    gather.handed(0)
+    work = pieces(triple.shape[1] // width, 3, project) + pieces(wins.shape[0] // area, 2, attend)
+    work += [restore_all] + pieces(features // width, 3, settle) + pieces(own // block, 2, norm_again)
+    spread(work, until(2))
+    gather.handed(2)
+    spread(pieces(hidden.shape[1] // width, 2, lift), until(3))
+    gather.handed(3)
     spread(pieces(features // width, features // width, lower), [])
     gather.drain()
 

time: 188 us -> 154 us (0.82)
  Pallas kernels: 178 us -> 143 us
    pallas_call x1, Pallas kernels: 178 us -> 143 us  [local(): pl.pallas_call(functools.partial(kernel, batches, 32, area), out_shape=ja...]
where the time goes in v3:
time: 154 us; the launch traced here: 153 us
  Pallas kernels  143 us (93%)
  local copies, waits for them, and re-layouts  4.88 us (3%)
  other arithmetic  3.72 us (2%)
    pallas_call x1, Pallas kernels, local(): pl.pallas_call(functools.partial(kernel, batches, 32, area), out_shape=ja...  143 us

profile of v3, /device:TPU:5, one launch (start us, length us, event | category | flops | bytes accessed | tf_op | source)
XLA Modules:
  0.0 152.9 jit_solution(17010101646234898607)
XLA Ops:
  0.0 0.0 copy-start
  0.0 0.0 copy-start.1
  0.1 0.1 reshape.223
  0.1 0.1 reshape.222
  0.2 0.1 concatenate.28
  0.3 0.1 concatenate.27
  0.4 0.1 add.65
  0.5 0.8 broadcast_add_fusion
  1.3 0.1 concatenate.26
  1.3 0.1 pad_add_fusion.3
  1.4 0.1 broadcast_add_fusion.1
  1.5 0.7 broadcast_subtract_fusion
  2.2 0.1 reshape.221
  2.3 0.1 reshape.220
  2.4 0.1 pad_add_fusion
  2.5 0.1 pad_add_fusion.1
  2.6 0.1 broadcast_compare_fusion.1
  2.7 0.1 broadcast_compare_fusion
  2.8 0.0 copy-done
  2.8 0.9 fusion
  3.7 0.7 copy.13.mod_ref
  4.4 0.8 and_convert_fusion.1.gather_out_ref
  5.2 0.9 and_convert_fusion.gather_in_ref
  6.1 0.0 copy-done.1
  6.1 1.1 fusion.6
  7.2 143.3 %shard_map.91 = bf16[384,1536]{1,0:T(8,128)(2,1)} custom-call(bf16[384,1536]{1,0:T(8,128)(2,1)} %bitcast.22, bf16[192,1536]{1,0:T(8,128)(2,1)} %bitcast.25, bf16[192,1536]{1,0:T(8,128)(2,1)} %bitcast.24, f32[3,6,1536]{2,1,0:T(8,128)} %copy.13.mod_ref, bf16[3,192,256]{2,1,0:T(8,128)(2,1)} %and_convert_fusion.gather_in_ref, ...), custom_call_target="tpu_custom_call" | custom-call | tf_op jit(solution)/shard_map/pallas_call | solution.py:462
  150.6 2.4 %copy.24 = bf16[3,8,16,1536]{3,2,1,0:T(8,128)(2,1)} copy(bf16[3,8,16,1536]{3,2,1,0:T(8,128)(2,1)} %bitcast.23) | data formatting | bytes 2359296
  (12 shorter events, 0.0 us)
Async XLA Ops:
  0.0 2.8 %copy-start = (bf16[32,6,1536]{2,0,1:T(8,128)(2,1)S(1)}, bf16[32,6,1536]{2,0,1:T(8,128)(2,1)}, u32[]{:S(2)}) copy-start(bf16[32,6,1536]{2,0,1:T(8,128)(2,1)} %param.12) | copy-start | bytes 1769476
  0.0 6.1 %copy-start.1 = (bf16[3,8,16,1536]{3,2,1,0:T(8,128)(2,1)S(1)}, bf16[3,8,16,1536]{3,2,1,0:T(8,128)(2,1)}, u32[]{:S(2)}) copy-start(bf16[3,8,16,1536]{3,2,1,0:T(8,128)(2,1)} %param.9) | copy-start | bytes 3538948

commit v4 on v3

--- a/solution.py
+++ b/solution.py
@@ -284,6 +284,7 @@
     me, count = lax.axis_index("win"), lax.axis_size("win")
     right, left = {"win": lax.rem(me + 1, count)}, {"win": lax.rem(me + count - 1, count)}
     meet(gather.neighbours() + [right, left])
+    gather.own(0)
     halos = []
     for at, src, dst, to in ((0, high_ref, prev, right), (1, low_ref, after, left)):
         made = pltpu.make_async_remote_copy(
@@ -296,7 +297,6 @@
         )
         made.start()
         halos.append(made)
-    gather.own(0)
     gather.own(1)
 
     def norm_into(src, first, dst, start, m, scale, shift):

time: 154 us -> 154 us (level)
  no operation moved by 1% of the time
where the time goes in v4:
time: 154 us; the launch traced here: 153 us
  Pallas kernels  144 us (94%)
  local copies, waits for them, and re-layouts  4.88 us (3%)
  other arithmetic  3.72 us (2%)
    pallas_call x1, Pallas kernels, local(): pl.pallas_call(functools.partial(kernel, batches, 32, area), out_shape=ja...  144 us

profile of v4, /device:TPU:5, one launch (start us, length us, event | category | flops | bytes accessed | tf_op | source)
XLA Modules:
  0.0 153.3 jit_solution(16082922704110511328)
XLA Ops:
  0.0 0.0 copy-start
  0.0 0.0 copy-start.1
  0.1 0.1 reshape.223
  0.1 0.1 reshape.222
  0.2 0.1 concatenate.28
  0.3 0.1 concatenate.27
  0.4 0.1 add.65
  0.5 0.8 broadcast_add_fusion
  1.3 0.1 concatenate.26
  1.3 0.1 pad_add_fusion.3
  1.4 0.1 broadcast_add_fusion.1
  1.5 0.7 broadcast_subtract_fusion
  2.2 0.1 reshape.221
  2.3 0.1 reshape.220
  2.4 0.1 pad_add_fusion
  2.5 0.1 pad_add_fusion.1
  2.6 0.1 broadcast_compare_fusion.1
  2.7 0.1 broadcast_compare_fusion
  2.8 0.0 copy-done
  2.8 0.9 fusion
  3.7 0.7 copy.13.mod_ref
  4.4 0.8 and_convert_fusion.1.gather_out_ref
  5.2 0.9 and_convert_fusion.gather_in_ref
  6.1 0.0 copy-done.1
  6.1 1.1 fusion.6
  7.2 143.7 %shard_map.91 = bf16[384,1536]{1,0:T(8,128)(2,1)} custom-call(bf16[384,1536]{1,0:T(8,128)(2,1)} %bitcast.22, bf16[192,1536]{1,0:T(8,128)(2,1)} %bitcast.25, bf16[192,1536]{1,0:T(8,128)(2,1)} %bitcast.24, f32[3,6,1536]{2,1,0:T(8,128)} %copy.13.mod_ref, bf16[3,192,256]{2,1,0:T(8,128)(2,1)} %and_convert_fusion.gather_in_ref, ...), custom_call_target="tpu_custom_call" | custom-call | tf_op jit(solution)/shard_map/pallas_call | solution.py:462
  151.0 2.4 %copy.24 = bf16[3,8,16,1536]{3,2,1,0:T(8,128)(2,1)} copy(bf16[3,8,16,1536]{3,2,1,0:T(8,128)(2,1)} %bitcast.23) | data formatting | bytes 2359296
  (12 shorter events, 0.0 us)
Async XLA Ops:
  0.0 2.8 %copy-start = (bf16[32,6,1536]{2,0,1:T(8,128)(2,1)S(1)}, bf16[32,6,1536]{2,0,1:T(8,128)(2,1)}, u32[]{:S(2)}) copy-start(bf16[32,6,1536]{2,0,1:T(8,128)(2,1)} %param.12) | copy-start | bytes 1769476
  0.0 6.1 %copy-start.1 = (bf16[3,8,16,1536]{3,2,1,0:T(8,128)(2,1)S(1)}, bf16[3,8,16,1536]{3,2,1,0:T(8,128)(2,1)}, u32[]{:S(2)}) copy-start(bf16[3,8,16,1536]{3,2,1,0:T(8,128)(2,1)} %param.9) | copy-start | bytes 3538948
